TPU v7x, 32 devices: a whole 2x2x4 slice. The times are simulated.
32 devices in a mesh: parts: 2 (over y), set: 4 (over x, core), seq: 4 (over z).
Axes of the slice: x: 2, y: 2, z: 4, core: 2. Of those that a mesh axis runs over, the one named last changes fastest.
Arguments:
- span_hidden: bfloat16 [512, 8192], P('parts', 'seq'), parts along dimension 0, may hold values from -500 to 500
- norm_gain: bfloat16 [8192], P('seq'), may hold values from 0.099609375 to 1.8984375
- key_value_weight: bfloat16 [8192, 2048], P('seq', 'set'), may hold values from -0.0625 to 0.0625
- prompt_key_value: bfloat16 [256, 2048], P(('parts', 'seq')), parts along dimension 0, may hold values from -6 to 6
- span_offset: int32 [2], P('parts'), parts along dimension 0, may hold values from 64 to 128
- cont_query: bfloat16 [32, 64, 8192], P(('parts', 'set', 'seq')), parts along dimension 0, may hold values from -24 to 24
- continuation_key_value: bfloat16 [32, 64, 2048], P(('parts', 'set', 'seq')), parts along dimension 0, may hold values from -6 to 6
- cont_lengths: int32 [32], P(('parts', 'set', 'seq')), parts along dimension 0, may hold values from 1 to 64
Outputs:
- span_key_value: bfloat16 [512, 2048], P(('parts', 'seq'), 'set'), parts along dimension 0
- attended: bfloat16 [32, 64, 8192], P(('parts', 'set', 'seq')), parts along dimension 0
There are 2 independent parts, one for each index of `parts`. A program takes and returns all parts, laid end to end along the dimension named above; an argument that names none is the same for every part. Nothing has to cross between parts.
All inputs are finite; a program needn't handle non-finite values.
Results may differ from a plain program's by a relative error of at most 0.02.
Values may be sent and summed in bfloat16 or wider, within the bound.
A program may use at most 64 MiB of HBM per device.

v0:
```python
import math

import jax
import jax.numpy as jnp
from jax import lax
from jax.sharding import PartitionSpec as P

MODEL_WIDTH = 8192
QUERY_HEADS = 64
KEY_HEADS = 8
HEAD_SIZE = 128
SPAN_LENGTH = 256


EPS = 1e-05
NEGATIVE_LARGE = -1e30


def frequencies(count, width, dtype):
    base = 500000.0 ** (-(jnp.arange(count).astype(dtype) * 2.0) / width)
    wave = 2.0 * math.pi / base
    smooth = (8192.0 / wave - 1.0) / 3.0
    blended = (1.0 - smooth) * base / 8.0 + smooth * base
    return jnp.where(wave < 2048.0, base, jnp.where(wave > 8192.0, base / 8.0, blended))


def apply_rotary(value_matrix, positions):
    mid_point = value_matrix.shape[-1] // 2
    frequency = frequencies(mid_point, value_matrix.shape[-1], value_matrix.dtype)
    angles = positions.astype(value_matrix.dtype)[:, None] * frequency[None, :]
    cosine = jnp.concatenate([jnp.cos(angles), jnp.cos(angles)], -1)[:, None, :]
    sine_part = jnp.concatenate([jnp.sin(angles), jnp.sin(angles)], -1)[:, None, :]
    turned = jnp.concatenate([-value_matrix[..., mid_point:], value_matrix[..., :mid_point]], -1)
    return value_matrix * cosine + turned * sine_part


def attend(state, query_rows, key_matrix, value_matrix, valid):
    best, total, accum = state
    scores = jnp.einsum(
        "tgkd,ngd->tgkn", query_rows, key_matrix, preferred_element_type=jnp.float32
    ) * HEAD_SIZE ** (-0.5)
    valid_four = valid.reshape(valid.shape[0], 1, 1, valid.shape[1])
    masked = jnp.where(valid_four, scores, NEGATIVE_LARGE)
    new_best = jnp.maximum(best, jnp.max(masked, axis=-1))
    weights = jnp.where(valid_four, jnp.exp(masked - new_best[..., None]), 0.0)
    shrink = jnp.exp(best - new_best)
    total = total * shrink + jnp.sum(weights, axis=-1)
    accum = accum * shrink[..., None] + jnp.einsum(
        "tgkn,ngd->tgkd",
        weights.astype(jnp.bfloat16),
        value_matrix,
        preferred_element_type=jnp.float32,
    )
    return (new_best, total, accum)


def attend_rows(state, query_rows, slice_part, valid_rows):
    sequence_length = slice_part.shape[0]
    key_columns_width = KEY_HEADS * HEAD_SIZE
    key_matrix = slice_part[:, :key_columns_width].reshape(sequence_length, KEY_HEADS, HEAD_SIZE)
    value_matrix = slice_part[:, key_columns_width:].reshape(sequence_length, KEY_HEADS, HEAD_SIZE)
    if sequence_length <= 256 or sequence_length % 256 != 0:
        return attend(state, query_rows, key_matrix, value_matrix, valid_rows[None, :])

    def one_block(index, inner):
        begin = index * 256
        block_keys = lax.dynamic_slice_in_dim(key_matrix, begin, 256, 0)
        block_values = lax.dynamic_slice_in_dim(value_matrix, begin, 256, 0)
        block_valid = lax.dynamic_slice_in_dim(valid_rows, begin, 256, 0)
        return attend(inner, query_rows, block_keys, block_values, block_valid[None, :])

    return lax.fori_loop(0, sequence_length // 256, one_block, state)


def on_device(
    span_hidden,
    norm_gain,
    key_value_weight,
    prompt_key_value,
    span_offset,
    cont_query,
    continuation_key_value,
    cont_lengths,
):
    offset = span_offset[0]
    key_columns_width = KEY_HEADS * HEAD_SIZE
    group_factor = QUERY_HEADS // KEY_HEADS
    span_rows = span_hidden.shape[0] // lax.axis_size("seq")
    hidden = span_hidden.astype(jnp.float32)
    squares = lax.psum(jnp.sum(hidden * hidden, axis=1), "seq")
    normed = (
        hidden
        * lax.rsqrt(squares / MODEL_WIDTH + EPS)[:, None]
        * norm_gain.astype(jnp.float32)[None, :]
    ).astype(jnp.bfloat16)
    block = lax.psum_scatter(
        jnp.dot(normed, key_value_weight, preferred_element_type=jnp.float32).astype(jnp.bfloat16),
        "seq",
        scatter_dimension=0,
        tiled=True,
    ).astype(jnp.float32)
    width = key_value_weight.shape[1]
    col_start = lax.axis_index("set") * width
    row_pos = offset + lax.axis_index("seq") * span_rows + jnp.arange(span_rows, dtype=jnp.int32)
    turned = apply_rotary(block.reshape(span_rows, width // HEAD_SIZE, HEAD_SIZE), row_pos).reshape(
        span_rows, width
    )
    block_kv = jnp.where(col_start < key_columns_width, turned, block).astype(jnp.bfloat16)
    step_length = cont_query.shape[1]
    token_index = jnp.arange(step_length, dtype=jnp.int32)
    self_positions = offset + SPAN_LENGTH + token_index
    query_rows = apply_rotary(
        cont_query[0].astype(jnp.float32).reshape(step_length, QUERY_HEADS, HEAD_SIZE),
        self_positions,
    ).astype(jnp.bfloat16)
    query_rows = query_rows.reshape(step_length, KEY_HEADS, group_factor, HEAD_SIZE)
    self_key_rows = apply_rotary(
        continuation_key_value[0, :, :key_columns_width]
        .astype(jnp.float32)
        .reshape(step_length, KEY_HEADS, HEAD_SIZE),
        self_positions,
    ).astype(jnp.bfloat16)
    self_value_rows = continuation_key_value[0, :, key_columns_width:].reshape(
        step_length, KEY_HEADS, HEAD_SIZE
    )
    state = (
        jnp.full((step_length, KEY_HEADS, group_factor), NEGATIVE_LARGE, jnp.float32),
        jnp.zeros((step_length, KEY_HEADS, group_factor), jnp.float32),
        jnp.zeros((step_length, KEY_HEADS, group_factor, HEAD_SIZE), jnp.float32),
    )
    causal = token_index[:, None] >= token_index[None, :]
    state = attend(state, query_rows, self_key_rows, self_value_rows, causal)
    joined_rows = lax.all_gather(block_kv, "set", axis=1, tiled=True)
    local_rows = jnp.concatenate([prompt_key_value, joined_rows], 0)
    cache_rows = prompt_key_value.shape[0]
    shard_rows = local_rows.shape[0]
    slice_part = lax.all_gather(local_rows, "seq", axis=0, tiled=True)
    global_row = jnp.arange(slice_part.shape[0], dtype=jnp.int32)
    within = global_row % shard_rows
    rows_valid = (within >= cache_rows) | (global_row // shard_rows * cache_rows + within < offset)
    state = attend_rows(state, query_rows, slice_part, rows_valid)
    best, total, accum = state
    mixed = (accum / total[..., None]).reshape(step_length, QUERY_HEADS * HEAD_SIZE)
    live = token_index < cont_lengths[0]
    attended = jnp.where(live[:, None], mixed, 0.0).astype(jnp.bfloat16)[None]
    return (block_kv, attended)


def solution(mesh):
    placed = (
        P("parts", "seq"),
        P("seq"),
        P("seq", "set"),
        P(("parts", "seq"), None),
        P("parts"),
        P(("parts", "set", "seq"), None, None),
        P(("parts", "set", "seq"), None, None),
        P(("parts", "set", "seq")),
    )
    return jax.shard_map(
        on_device,
        mesh=mesh,
        in_specs=placed,
        out_specs=(P(("parts", "seq"), "set"), P(("parts", "set", "seq"), None, None)),
        check_vma=False,
    )
```

profile of v0, /device:TPU:1, one launch (start us, length us, event | category | flops | bytes accessed | tf_op | source)
XLA Modules:
  0.0 119.9 jit_solution(6057361284964646912)
XLA Ops:
  7.2 0.0 copy-start
  7.2 0.0 reduce-scatter.2.cloned.1.call-start
  7.2 1.6 %fusion.6 = f32[256]{0:T(256)S(1)} fusion(bf16[256,2048]{1,0:T(8,128)(2,1)} %param.8), kind=kLoop, calls=%fused_computation.11 | loop fusion | flops 1572608 | bytes 1049600 | tf_op jit(solution)/shard_map/reduce_sum | solution.py:90
  8.9 10.8 %psum.7 = f32[256]{0:T(256)S(1)} all-reduce(f32[256]{0:T(256)S(1)} %fusion.6), channel_id=1, replica_groups=mesh['parts'=2,'set'=4,'seq'=4] {'seq'}, use_global_device_ids=true, to_apply=%region_1.0 | all-reduce | flops 256 | bytes 2048 | tf_op jit(solution)/shard_map/psum | solution.py:90
  19.6 0.7 convert_element_type.88
  20.3 2.7 %convolution_convert_fusion = bf16[256,512]{1,0:T(8,128)(2,1)} fusion(bf16[2048,512]{1,0:T(8,128)(2,1)S(1)} %copy-done, bf16[256,2048]{1,0:T(8,128)(2,1)} %param.8, f32[2048]{0:T(1024)S(1)} %convert_element_type.88, f32[256]{0:T(256)S(1)} %add_rsqrt_fusion), kind=kOutput, calls=%fused_computation.30 | convolution fusion | flops 539099136 | bytes 3417088 | tf_op jit(solution)/shard_map/dot_general | solution.py:97
  23.0 0.0 reduce-scatter.2.cloned.1.call-update
  23.0 0.0 all-gather.2.cloned.1.call-start
  23.8 0.3 multiply_cosine_fusion
  24.1 0.1 pad_maximum_fusion.1
  24.2 16.9 %reduce-scatter.2.cloned.1.call-done = bf16[64,512]{1,0:T(8,128)(2,1)} async-done(((bf16[256,512]{1,0:T(8,128)(2,1)}), bf16[64,512]{1,0:T(8,128)(2,1)}) %reduce-scatter.2.cloned.1.call-update) | async-done | bytes 65552 | tf_op jit(solution)/shard_map/reduce_scatter | solution.py:96
  41.1 0.9 reshape.175
  42.0 0.1 slice_negate_fusion.2
  42.1 0.1 maximum_multiply_fusion.2
  42.3 1.0 fusion.30
  43.3 0.6 copy-done.5
  43.9 8.7 %all_gather.6 = bf16[64,2048]{1,0:T(8,128)(2,1)S(1)} all-gather(bf16[64,512]{1,0:T(8,128)(2,1)S(1)} %fusion.30), channel_id=1, replica_groups=mesh['parts'=2,'set'=4,'seq'=4] {'set'}, dimensions={1}, use_global_device_ids=true | all-gather | bytes 327680 | tf_op jit(solution)/shard_map/all_gather | solution.py:133
  52.6 1.7 %pad_maximum_fusion = bf16[96,2048]{1,0:T(8,128)(2,1)} fusion(bf16[64,2048]{1,0:T(8,128)(2,1)S(1)} %all_gather.6, bf16[32,2048]{1,0:T(8,128)(2,1)} %param.11), kind=kLoop, calls=%fused_computation.38 | loop fusion | flops 786432 | bytes 786432 | tf_op jit(solution)/shard_map/concatenate | solution.py:134
  54.3 0.0 all-gather.2.cloned.1.call-update
  55.1 0.1 copy.23
  55.1 0.1 convert_bitcast_fusion
  55.3 0.4 copy.53
  55.7 0.9 slice_negate_fusion
  56.5 1.2 %copy.27 = f32[64,64,64]{2,0,1:T(8,128)S(1)} copy(f32[64,64,64]{2,1,0:T(8,128)S(1)} %get-tuple-element.8) | data formatting | bytes 2097152 | tf_op jit(solution)/shard_map/neg | solution.py:33
  57.8 1.2 %copy.28 = f32[64,64,64]{2,0,1:T(8,128)S(1)} copy(f32[64,64,64]{2,1,0:T(8,128)S(1)} %get-tuple-element.9) | data formatting | bytes 2097152 | tf_op jit(solution)/shard_map/slice | solution.py:33
  59.0 0.1 pad_maximum_fusion.3
  59.1 0.1 slice_negate_fusion.1
  59.3 1.5 %fusion.10 = bf16[64,8,8,128]{3,0,2,1:T(8,128)(2,1)S(1)} fusion(f32[64,8,8,64]{3,0,2,1:T(8,128)S(1)} %bitcast.95, f32[64,8,8,64]{3,0,2,1:T(8,128)S(1)} %bitcast.94, f32[64,8,8,128]{3,2,1,0:T(8,128)S(1)} %bitcast.93, f32[64,128]{1,0:T(8,128)S(1)} %get-tuple-element.34, f32[64,128]{1,0:T(8,128)S(1)} %get-tuple-element.33), kind=kLoop, calls=%fused_computation.17 | loop fusion | flops 2621440 | bytes 5308416 | tf_op jit(solution)/shard_map/convert_element_type | solution.py:115
  60.7 2.5 %fusion.13 = (f32[64,8,8]{0,2,1:T(8,128)S(1)}, f32[8,64,64,8]{2,1,3,0:T(8,128)}) fusion(pred[64,64]{0,1:T(8,128)(4,1)S(1)} %iota_compare_fusion, bf16[64,8,8,128]{3,0,2,1:T(8,128)(2,1)S(1)} %fusion.10, f32[64,8,64]{2,0,1:T(8,128)S(1)} %get-tuple-element.15, f32[64,8,64]{2,0,1:T(8,128)S(1)} %get-tuple-element.14, f32[64,128]{1,0:T(8,128)S(1)} %get-tuple-element.34, ...), kind=kOutput, calls=%fused_computation.27 | convolution fusion | flops 68218880 | bytes 2707456 | tf_op jit(solution)/shard_map/tgkd,ngd->tgkn/dot_general | solution.py:39
  63.2 25.0 %all-gather.2.cloned.1.call-done = bf16[384,2048]{1,0:T(8,128)(2,1)} async-done(((bf16[96,2048]{1,0:T(8,128)(2,1)}), bf16[384,2048]{1,0:T(8,128)(2,1)}) %all-gather.2.cloned.1.call-update) | async-done | bytes 1572880 | tf_op jit(solution)/shard_map/all_gather | solution.py:137
  88.3 1.5 %slice_bitcast_fusion = (bf16[48,8,8,128]{3,1,2,0:T(8,128)(2,1)S(1)}, bf16[48,8,8,128]{3,1,2,0:T(8,128)(2,1)S(1)}) fusion(bf16[384,2048]{1,0:T(8,128)(2,1)} %all-gather.2.cloned.1.call-done), kind=kLoop, calls=%fused_computation.33 | loop fusion | bytes 3145728
  89.8 1.1 copy.57
  90.8 0.2 copy.56
  91.0 1.2 bitcast_reduce_fusion
  92.2 0.6 exponential_multiply_fusion
  92.8 0.8 fusion.16
  93.6 3.3 %fusion.2 = (f32[64,8,8]{0,2,1:T(8,128)S(1)}, bf16[64,8,8,384]{3,0,2,1:T(8,128)(2,1)}) fusion(f32[8,384,64,8]{1,2,3,0:T(8,128)S(1)} %get-tuple-element.30, f32[64,8,8]{0,2,1:T(8,128)S(1)} %get-tuple-element.19, pred[384]{0:T(512)(128)(4,1)S(1)} %fusion.42), kind=kLoop, calls=%fused_computation.5 | loop fusion | flops 9433088 | bytes 9470336 | tf_op jit(solution)/shard_map/reduce_sum | solution.py:47
  96.9 0.6 multiply_add_fusion
  97.5 0.9 copy.36
  98.4 1.6 %copy.29 = f32[64,8,8]{2,0,1:T(8,128)} copy(f32[64,8,8]{0,2,1:T(8,128)} %get-tuple-element.18) | data formatting | bytes 32768 | tf_op jit(solution)/shard_map/mul;broadcast_in_dim | solution.py:48
  100.0 1.6 %copy.33 = f32[64,8,8]{2,0,1:T(8,128)} copy(f32[64,8,8]{0,2,1:T(8,128)} %get-tuple-element.3) | data formatting | bytes 32768 | tf_op jit(solution)/shard_map/exp | solution.py:46
  101.6 1.5 %copy.30 = bf16[64,8,8,64]{3,2,0,1:T(8,128)(2,1)} copy(bf16[64,8,8,64]{0,3,2,1:T(8,128)(2,1)S(1)} %get-tuple-element.7) | data formatting | bytes 1048576 | tf_op jit(solution)/shard_map/convert_element_type | solution.py:50
  103.1 1.8 %fusion.31 = f32[8,64,8,128]{3,2,1,0:T(8,128)S(1)} fusion(bf16[64,8,8,64]{3,2,0,1:T(8,128)(2,1)} %copy.30, bf16[64,8,128,1]{2,1,0,3:T(8,128)(2,1)S(1)} %bitcast.100), kind=kOutput, calls=%fused_computation.52 | convolution fusion | flops 67108864 | bytes 2752512 | tf_op jit(solution)/shard_map/tgkn,ngd->tgkd/dot_general | solution.py:48
  104.9 0.4 copy-done.2
  105.3 3.8 %fusion.11 = bf16[64,8,8,128]{3,2,0,1:T(8,128)(2,1)S(1)} fusion(f32[8,64,8,128]{3,2,1,0:T(8,128)S(1)} %fusion.31, bf16[64,8,8,384]{3,0,2,1:T(8,128)(2,1)S(1)} %copy-done.2, f32[64,8,8]{2,0,1:T(8,128)S(1)} %copy.36, f32[64,8,8]{2,0,1:T(8,128)} %copy.33, f32[64,8,8]{2,0,1:T(8,128)} %copy.29, bf16[384,8,128,1]{2,1,0,3:T(8,128)(2,1)} %bitcast.99), kind=kOutput, calls=%fused_computation.19 | convolution fusion | flops 405274624 | bytes 7127040 | tf_op jit(solution)/shard_map/tgkn,ngd->tgkd/dot_general | solution.py:48
  109.0 1.3 %copy.37 = bf16[64,8,8,128]{3,2,1,0:T(8,128)(2,1)} copy(bf16[64,8,8,128]{3,2,0,1:T(8,128)(2,1)S(1)} %fusion.11) | data formatting | bytes 2097152 | tf_op jit(solution)/shard_map/div | solution.py:143
  110.3 1.5 %reshape.178 = bf16[1,64,8192]{2,1,0:T(8,128)(2,1)S(1)} reshape(bf16[64,8,8,128]{3,2,1,0:T(8,128)(2,1)} %copy.37) | data formatting | bytes 2097152 | tf_op jit(solution)/shard_map/reshape | solution.py:143
  111.8 1.2 %select_convert_fusion = bf16[1,64,8192]{2,1,0:T(8,128)(2,1)} fusion(bf16[1,64,8192]{2,1,0:T(8,128)(2,1)S(1)} %reshape.178, pred[64]{0:T(512)(128)(4,1)S(1)} %iota_compare_fusion.1), kind=kLoop, calls=%fused_computation.25 | loop fusion | flops 524288 | bytes 2097216 | tf_op jit(solution)/shard_map/convert_element_type | solution.py:145
  (20 shorter events, 0.2 us)
Async XLA Ops:
  7.2 13.2 %copy-start = (bf16[2048,512]{1,0:T(8,128)(2,1)S(1)}, bf16[2048,512]{1,0:T(8,128)(2,1)}, u32[]{:S(2)}) copy-start(bf16[2048,512]{1,0:T(8,128)(2,1)} %param.10) | copy-start | bytes 6291460
  7.2 33.9 %reduce-scatter.2.cloned.1.call-start = ((), (), s32[]{:S(2)}) async-start(), calls=%async_computation.1 | async-start | bytes 327680 | tf_op jit(solution)/shard_map/reduce_scatter | solution.py:96
  23.0 31.9 %copy-start.4 = (bf16[1,64,2048]{2,1,0:T(8,128)(2,1)S(1)}, bf16[1,64,2048]{2,1,0:T(8,128)(2,1)}, u32[]{:S(2)}) copy-start(bf16[1,64,2048]{2,1,0:T(8,128)(2,1)} %param.14) | copy-start | bytes 786436
  23.0 65.2 %all-gather.2.cloned.1.call-start = ((), (), s32[]{:S(2)}) async-start(), calls=%async_computation.2 | async-start | bytes 1966080 | tf_op jit(solution)/shard_map/all_gather | solution.py:137
  42.3 12.9 %copy-start.3 = (bf16[1,64,8192]{2,1,0:T(8,128)(2,1)S(1)}, bf16[1,64,8192]{2,1,0:T(8,128)(2,1)}, u32[]{:S(2)}) copy-start(bf16[1,64,8192]{2,1,0:T(8,128)(2,1)} %param.13) | copy-start | bytes 3145732
  43.3 0.6 copy-start.5
  91.0 1.8 %copy-start.1 = (f32[8,64,64,8]{2,1,3,0:T(8,128)S(1)}, f32[8,64,64,8]{2,1,3,0:T(8,128)}, u32[]{:S(2)}) copy-start(f32[8,64,64,8]{2,1,3,0:T(8,128)} %get-tuple-element.28) | copy-start | bytes 3145732
  103.1 2.2 %copy-start.2 = (bf16[64,8,8,384]{3,0,2,1:T(8,128)(2,1)S(1)}, bf16[64,8,8,384]{3,0,2,1:T(8,128)(2,1)}, u32[]{:S(2)}) copy-start(bf16[64,8,8,384]{3,0,2,1:T(8,128)(2,1)} %get-tuple-element.5) | copy-start | bytes 9437188
Sparse Core Ops, SparseCore 0:
  23.2 17.8 reduce-scatter.1
  54.4 33.8 all-gather.1
where the time goes:
time: 122 us; the launch traced here: 120 us
  waiting for transfers between devices  41.9 us (34%)
  blocking collectives  19.5 us (16%)
  local copies, waits for them, and re-layouts  15.9 us (13%)
  between operations  15.6 us (13%)
  other arithmetic  15 us (12%)
  matrix products  11.9 us (10%)
    all_gather x1, waiting for transfers between devices, on_device(): slice_part = lax.all_gather(local_rows, 'seq', axis=0, tiled=True)  25 us
    reduce_scatter x1, waiting for transfers between devices, on_device(): lax.psum_scatter(jnp.dot(normed, key_value_weight, preferred_element_type...  16.9 us
    psum x1, blocking collectives, on_device(): squares = lax.psum(jnp.sum(hidden * hidden, axis=1), 'seq')  10.8 us
    all_gather x1, blocking collectives, on_device(): joined_rows = lax.all_gather(block_kv, 'set', axis=1, tiled=True)  8.7 us
    dot_general x2, matrix products, attend(): jnp.einsum('tgkn,ngd->tgkd', weights.astype(jnp.bfloat16), value_matrix,...  5.55 us
    unnamed x18, local copies, waits for them, and re-layouts  4.21 us
    reduce_sum x2, other arithmetic, attend(): total = total * shrink + jnp.sum(weights, axis=-1)  4.09 us
    dot_general x2, matrix products, attend(): jnp.einsum('tgkd,ngd->tgkn', query_rows, key_matrix, preferred_element_ty...  3.66 us
  transfers between devices with their start and end apart: 2, of which 2 were waited for; matrix products, arithmetic and copies ran while one was open for 7% of the time, Pallas kernels for 0%

commit v1 on v0

v1 whole, which is shorter than its diff:
```python
import functools
import math

import jax
import jax.numpy as jnp
import numpy as np
from jax import lax
from jax.experimental import pallas as pl
from jax.experimental.pallas import tpu as pltpu
from jax.sharding import PartitionSpec as P

MODEL_WIDTH = 8192
QUERY_HEADS = 64
KEY_HEADS = 8
HEAD_SIZE = 128
SPAN_LENGTH = 256
GROUP = QUERY_HEADS // KEY_HEADS
KEY_COLUMNS = KEY_HEADS * HEAD_SIZE

EPS = 1e-05
NEGATIVE_LARGE = -1e30
EXPONENT = HEAD_SIZE ** (-0.5) * math.log2(math.e)

MESH = pl.DeviceIdType.MESH
F32 = jnp.float32
BF16 = jnp.bfloat16


def frequency_table():
    index = np.arange(HEAD_SIZE // 2, dtype=np.float64)
    base = 500000.0 ** (-2.0 * index / HEAD_SIZE)
    wave = 2.0 * np.pi / base
    smooth = (8192.0 / wave - 1.0) / 3.0
    blended = (1.0 - smooth) * base / 8.0 + smooth * base
    table = np.where(wave < 2048.0, base, np.where(wave > 8192.0, base / 8.0, blended))
    row = np.concatenate([table, table]).astype(np.float32)
    return np.broadcast_to(row, (8, HEAD_SIZE)).copy()


def rotary_tables(frequency, start, rows):
    positions = (start + lax.broadcasted_iota(jnp.int32, (rows, HEAD_SIZE), 0)).astype(F32)
    angles = positions * frequency
    lane = lax.broadcasted_iota(jnp.int32, (rows, HEAD_SIZE), 1)
    sine = jnp.sin(angles)
    return jnp.cos(angles), jnp.where(lane < HEAD_SIZE // 2, -sine, sine)


def turn(value, cosine, sine):
    return value * cosine + pltpu.roll(value, HEAD_SIZE // 2, 1) * sine


def scores_of(query, keys):
    return lax.dot_general(query, keys, (((1,), (1,)), ((), ())), preferred_element_type=F32)


def with_ones(values):
    return jnp.concatenate([values, jnp.ones_like(values)], axis=1)


def kernel(
    n_set,
    n_seq,
    hidden_hbm,
    gain_hbm,
    weight_hbm,
    prompt_hbm,
    offset_smem,
    query_hbm,
    own_hbm,
    frequency_hbm,
    span_out,
    attended_out,
    hidden,
    gain,
    weight,
    prompt,
    query_in,
    own,
    frequency,
    scaled,
    partial,
    sending,
    received,
    square_mine,
    square_theirs,
    square_column,
    span,
    query,
    best,
    accum,
    load_sem,
    span_store_sem,
    square_send,
    square_recv,
    part_send,
    part_recv,
    pz_send,
    pz_recv,
    px_send,
    px_recv,
    pc_send,
    pc_recv,
    sz_send,
    sz_recv,
    sx_send,
    sx_recv,
    sc_send,
    sc_recv,
):
    n_x = n_set // 2
    me_set = lax.axis_index("set")
    me_seq = lax.axis_index("seq")
    me_x, me_core = me_set // 2, me_set % 2
    width = weight.shape[1]
    rows = span.shape[1] // n_seq
    cached = prompt.shape[1] // n_seq
    tokens = query_in.shape[0]
    halves = 2 if width % 512 == 0 else 1
    half = width // halves

    def seq_at(step):
        return (me_seq + step) % n_seq

    def set_at(step):
        return ((me_x + step) % n_x) * 2 + me_core

    twin = me_x * 2 + 1 - me_core

    def rows_of(which, count):
        return pl.ds(pl.multiple_of(which * count, count), count)

    loads = []

    def load(source, target):
        copy = pltpu.make_async_copy(source, target, load_sem.at[len(loads)])
        copy.start()
        loads.append(copy)
        return copy

    prompt_loads = [
        load(
            prompt_hbm.at[:, pl.ds(s * width, width)],
            prompt.at[s, rows_of(me_seq, cached), :],
        )
        for s in range(n_set)
    ]
    hidden_load = load(hidden_hbm, hidden)
    gain_load = load(gain_hbm, gain)
    weight_loads = [
        load(weight_hbm.at[:, pl.ds(i * half, half)], weight.at[:, pl.ds(i * half, half)])
        for i in range(halves)
    ]
    frequency_load = load(frequency_hbm, frequency)
    own_load = load(own_hbm.at[0], own)
    query_load = load(query_hbm.at[0], query_in)

    barrier = pltpu.get_barrier_semaphore()
    partners = [{"seq": seq_at(d)} for d in range(1, n_seq)]
    partners += [{"set": set_at(d)} for d in range(1, n_x)]
    partners += [{"set": twin}]
    for partner in partners:
        pl.semaphore_signal(barrier, inc=1, device_id=partner, device_id_type=MESH)

    hidden_load.wait()
    gain_load.wait()
    squares = jnp.zeros((hidden.shape[0], HEAD_SIZE), F32)
    for i in range(hidden.shape[1] // HEAD_SIZE):
        block = hidden[:, i * HEAD_SIZE : (i + 1) * HEAD_SIZE].astype(F32)
        squares += block * block
        scaled[:, i * HEAD_SIZE : (i + 1) * HEAD_SIZE] = (
            block * gain[i : i + 1, :].astype(F32)
        ).astype(BF16)
    square_row = jnp.sum(squares.T, axis=0, keepdims=True)
    square_mine[...] = jnp.broadcast_to(square_row, square_mine.shape)

    for copy in prompt_loads:
        copy.wait()
    pl.semaphore_wait(barrier, len(partners))

    copies = []

    def send(source, target, send_sem, recv_sem, device):
        copy = pltpu.make_async_remote_copy(
            src_ref=source,
            dst_ref=target,
            send_sem=send_sem,
            recv_sem=recv_sem,
            device_id=device,
            device_id_type=MESH,
        )
        copy.start()
        copies.append(copy)
        return copy

    def prompt_block(s, z):
        return prompt.at[s, rows_of(z, cached), :]

    def span_block(s, z):
        return span.at[s, rows_of(z, rows), :]

    prompt_z = []
    for d in range(1, n_seq):
        block = prompt_block(me_set, me_seq)
        prompt_z.append(
            send(block, block, pz_send.at[d], pz_recv.at[d], {"seq": seq_at(d)})
        )
    square_copies = [
        send(
            square_mine,
            square_theirs.at[d],
            square_send.at[d],
            square_recv.at[d],
            {"seq": seq_at(d)},
        )
        for d in range(1, n_seq)
    ]

    part_copies = []
    for i in range(halves):
        weight_loads[i].wait()
        columns = pl.ds(i * half, half)
        product = jnp.dot(scaled[...], weight[:, columns], preferred_element_type=F32)
        partial[:, columns] = product
        sending[i] = product.astype(BF16)
        for d in range(1, n_seq):
            part_copies.append(
                send(
                    sending.at[i, rows_of(seq_at(d), rows), :],
                    received.at[i, d],
                    part_send.at[i, d],
                    part_recv.at[i, d],
                    {"seq": seq_at(d)},
                )
            )

    frequency_load.wait()
    offset = offset_smem[0]
    cosine, sine = rotary_tables(frequency[0:1, :], offset + SPAN_LENGTH, tokens)
    span_cosine, span_sine = rotary_tables(frequency[0:1, :], offset + me_seq * rows, rows)
    own_load.wait()
    query_load.wait()

    causal = jnp.concatenate(
        [
            lax.broadcasted_iota(jnp.int32, (tokens, tokens), 0)
            >= lax.broadcasted_iota(jnp.int32, (tokens, tokens), 1)
        ]
        * GROUP,
        axis=0,
    )

    def columns_of(head):
        return pl.ds(pl.multiple_of(head * HEAD_SIZE, HEAD_SIZE), HEAD_SIZE)

    def attend_own(head, carry):
        for g in range(GROUP):
            raw = query_in[:, columns_of(head * GROUP + g)].astype(F32)
            query[head, pl.ds(g * tokens, tokens), :] = turn(raw, cosine, sine).astype(BF16)
        keys = turn(own[:, columns_of(head)].astype(F32), cosine, sine).astype(BF16)
        values = own[:, columns_of(head + KEY_HEADS)]
        scores = jnp.where(causal, scores_of(query[head], keys), NEGATIVE_LARGE)
        top = jnp.max(scores, axis=1, keepdims=True)
        weights = jnp.exp2((scores - top) * EXPONENT).astype(BF16)
        best[head] = jnp.broadcast_to(top, best.shape[1:])
        accum[head] = jnp.dot(weights, with_ones(values), preferred_element_type=F32)
        return carry

    def pass_prompt(d):
        prompt_z[d - 1].wait_recv()
        block = prompt_block(me_set, seq_at(n_seq - d))
        for e in range(1, n_x):
            send(block, block, px_send.at[d, e], px_recv.at[d, e], {"set": set_at(e)})
        send(block, block, pc_send.at[d, 0], pc_recv.at[d, 0], {"set": twin})

    def pass_prompt_twin(d):
        block = prompt_block(me_set, seq_at(n_seq - d))
        for e in range(1, n_x):
            pltpu.make_async_remote_copy(
                block, block, px_send.at[d, e], px_recv.at[d, e], {"set": set_at(e)}, MESH
            ).wait_recv()
            come = prompt_block(set_at(n_x - e), seq_at(n_seq - d))
            send(come, come, pc_send.at[d, e], pc_recv.at[d, e], {"set": twin})

    lax.fori_loop(0, KEY_HEADS // 4, attend_own, 0)
    for d in range(1, n_seq):
        pass_prompt(d)
    lax.fori_loop(KEY_HEADS // 4, KEY_HEADS, attend_own, 0)
    for d in range(1, n_seq):
        pass_prompt_twin(d)

    for copy in square_copies:
        copy.wait_recv()
    square_total = square_mine[...]
    for d in range(1, n_seq):
        square_total += square_theirs[d]
    square_column[...] = jnp.broadcast_to(
        square_total[0:1, :], (HEAD_SIZE, square_total.shape[1])
    ).T
    inverse = lax.rsqrt(square_column[rows_of(me_seq, rows), :] / MODEL_WIDTH + EPS)
    for copy in part_copies:
        copy.wait_recv()
    for i in range(halves):
        for j in range(half // HEAD_SIZE):
            column = i * half + j * HEAD_SIZE
            block = partial[rows_of(me_seq, rows), pl.ds(column, HEAD_SIZE)]
            for d in range(1, n_seq):
                block += received[i, d, :, pl.ds(j * HEAD_SIZE, HEAD_SIZE)].astype(F32)
            block = block * inverse
            turned = turn(block, span_cosine, span_sine)
            is_key = me_set * width + column < KEY_COLUMNS
            span[me_set, rows_of(me_seq, rows), pl.ds(column, HEAD_SIZE)] = jnp.where(
                is_key, turned, block
            ).astype(BF16)

    mine = span_block(me_set, me_seq)
    span_z = []
    sx, sc = {}, {}
    for e in range(1, n_x):
        sx[0, e] = send(mine, mine, sx_send.at[0, e], sx_recv.at[0, e], {"set": set_at(e)})
    for d in range(1, n_seq):
        span_z.append(send(mine, mine, sz_send.at[d], sz_recv.at[d], {"seq": seq_at(d)}))
    send(mine, mine, sc_send.at[0, 0], sc_recv.at[0, 0], {"set": twin})
    span_store = pltpu.make_async_copy(mine, span_out, span_store_sem)
    span_store.start()

    def pass_span(d):
        span_z[d - 1].wait_recv()
        block = span_block(me_set, seq_at(n_seq - d))
        for e in range(1, n_x):
            sx[d, e] = send(
                block, block, sx_send.at[d, e], sx_recv.at[d, e], {"set": set_at(e)}
            )
        send(block, block, sc_send.at[d, 0], sc_recv.at[d, 0], {"set": twin})

    def pass_span_twin(d):
        for e in range(1, n_x):
            sx[d, e].wait_recv()
            come = span_block(set_at(n_x - e), seq_at(n_seq - d))
            send(come, come, sc_send.at[d, e], sc_recv.at[d, e], {"set": twin})

    def attend_more(head, keys, values, mask):
        scores = scores_of(query[head], keys)
        if mask is not None:
            scores = jnp.where(mask, scores, NEGATIVE_LARGE)
        old = best[head][:, 0:1]
        top = jnp.maximum(old, jnp.max(scores, axis=1, keepdims=True))
        weights = jnp.exp2((scores - top) * EXPONENT).astype(BF16)
        shrink = jnp.exp2((old - top) * EXPONENT)
        total = accum[head] * shrink + jnp.dot(
            weights, with_ones(values), preferred_element_type=F32
        )
        return top, total

    per_set = width // HEAD_SIZE

    def head_of(array, head):
        return array[head // per_set, :, columns_of(head % per_set)]

    live = (
        lax.broadcasted_iota(jnp.int32, (1, prompt.shape[1]), 1) < offset
    )

    def attend_prompt(head, carry):
        top, total = attend_more(
            head, head_of(prompt, head), head_of(prompt, head + KEY_HEADS), live
        )
        best[head] = jnp.broadcast_to(top, best.shape[1:])
        accum[head] = total
        return carry

    for d in range(1, n_seq):
        for e in range(n_x):
            pltpu.make_async_remote_copy(
                prompt_block(me_set, me_seq),
                prompt_block(me_set, me_seq),
                pc_send.at[d, e],
                pc_recv.at[d, e],
                {"set": twin},
                MESH,
            ).wait_recv()
    cut = [KEY_HEADS * d // n_seq for d in range(n_seq + 1)]
    lax.fori_loop(cut[0], cut[1], attend_prompt, 0)
    pass_span_twin(0)
    for d in range(1, n_seq):
        pass_span(d)
        if cut[d] < cut[d + 1]:
            lax.fori_loop(cut[d], cut[d + 1], attend_prompt, 0)
    for d in range(1, n_seq):
        pass_span_twin(d)
    for d in range(n_seq):
        for e in range(n_x):
            pltpu.make_async_remote_copy(
                mine, mine, sc_send.at[d, e], sc_recv.at[d, e], {"set": twin}, MESH
            ).wait_recv()

    def attend_span(head, carry):
        top, total = attend_more(
            head, head_of(span, head), head_of(span, head + KEY_HEADS), None
        )
        mixed = (total[:, :HEAD_SIZE] / total[:, HEAD_SIZE:]).astype(BF16)
        for g in range(GROUP):
            attended_out[:, columns_of(head * GROUP + g)] = mixed[
                g * tokens : (g + 1) * tokens, :
            ]
        return carry

    lax.fori_loop(0, KEY_HEADS, attend_span, 0)

    for copy in copies:
        copy.wait_send()
    span_store.wait()


def on_device(
    n_set,
    n_seq,
    span_hidden,
    norm_gain,
    key_value_weight,
    prompt_key_value,
    span_offset,
    cont_query,
    continuation_key_value,
    cont_lengths,
):
    span_length, features = span_hidden.shape
    width = key_value_weight.shape[1]
    rows = span_length // n_seq
    cached = prompt_key_value.shape[0]
    tokens = cont_query.shape[1]
    n_x = n_set // 2
    halves = 2 if width % 512 == 0 else 1
    half = width // halves
    frequency = jnp.asarray(frequency_table())
    gain = norm_gain.reshape(features // HEAD_SIZE, HEAD_SIZE)
    dma = pltpu.SemaphoreType.DMA
    anywhere = pl.BlockSpec(memory_space=pl.ANY)
    span_rows, attended = pl.pallas_call(
        functools.partial(kernel, n_set, n_seq),
        out_shape=(
            jax.ShapeDtypeStruct((rows, width), BF16),
            jax.ShapeDtypeStruct((tokens, QUERY_HEADS * HEAD_SIZE), BF16),
        ),
        in_specs=[
            anywhere,
            anywhere,
            anywhere,
            anywhere,
            pl.BlockSpec(memory_space=pltpu.SMEM),
            anywhere,
            anywhere,
            anywhere,
        ],
        out_specs=(anywhere, pl.BlockSpec(memory_space=pltpu.VMEM)),
        scratch_shapes=[
            pltpu.VMEM((span_length, features), BF16),
            pltpu.VMEM((features // HEAD_SIZE, HEAD_SIZE), BF16),
            pltpu.VMEM((features, width), BF16),
            pltpu.VMEM((n_set, cached * n_seq, width), BF16),
            pltpu.VMEM((tokens, QUERY_HEADS * HEAD_SIZE), BF16),
            pltpu.VMEM((tokens, 2 * KEY_COLUMNS), BF16),
            pltpu.VMEM((8, HEAD_SIZE), F32),
            pltpu.VMEM((span_length, features), BF16),
            pltpu.VMEM((span_length, width), F32),
            pltpu.VMEM((halves, span_length, half), BF16),
            pltpu.VMEM((halves, n_seq, rows, half), BF16),
            pltpu.VMEM((8, span_length), F32),
            pltpu.VMEM((n_seq, 8, span_length), F32),
            pltpu.VMEM((span_length, HEAD_SIZE), F32),
            pltpu.VMEM((n_set, span_length, width), BF16),
            pltpu.VMEM((KEY_HEADS, GROUP * tokens, HEAD_SIZE), BF16),
            pltpu.VMEM((KEY_HEADS, GROUP * tokens, HEAD_SIZE), F32),
            pltpu.VMEM((KEY_HEADS, GROUP * tokens, 2 * HEAD_SIZE), F32),
            dma((n_set + halves + 5,)),
            dma,
            dma((n_seq,)),
            dma((n_seq,)),
            dma((halves, n_seq)),
            dma((halves, n_seq)),
            dma((n_seq,)),
            dma((n_seq,)),
            dma((n_seq, n_x)),
            dma((n_seq, n_x)),
            dma((n_seq, n_x)),
            dma((n_seq, n_x)),
            dma((n_seq,)),
            dma((n_seq,)),
            dma((n_seq, n_x)),
            dma((n_seq, n_x)),
            dma((n_seq, n_x)),
            dma((n_seq, n_x)),
        ],
        compiler_params=pltpu.CompilerParams(
            collective_id=0, has_side_effects=True, vmem_limit_bytes=48 * 1024 * 1024
        ),
        name="project_gather_attend",
    )(
        span_hidden,
        gain,
        key_value_weight,
        prompt_key_value,
        span_offset,
        cont_query,
        continuation_key_value,
        frequency,
    )
    live = jnp.arange(tokens, dtype=jnp.int32) < cont_lengths[0]
    return span_rows, jnp.where(live[:, None], attended, 0.0).astype(BF16)[None]


def solution(mesh):
    placed = (
        P("parts", "seq"),
        P("seq"),
        P("seq", "set"),
        P(("parts", "seq"), None),
        P("parts"),
        P(("parts", "set", "seq"), None, None),
        P(("parts", "set", "seq"), None, None),
        P(("parts", "set", "seq")),
    )
    return jax.shard_map(
        functools.partial(on_device, mesh.shape["set"], mesh.shape["seq"]),
        mesh=mesh,
        in_specs=placed,
        out_specs=(P(("parts", "seq"), "set"), P(("parts", "set", "seq"), None, None)),
        check_vma=False,
    )
```

time: 122 us -> 46.8 us (0.38); the launches traced: 120 us -> 46.4 us
  waiting for transfers between devices: 41.9 us -> 0 us
  Pallas kernels: 0 us -> 35.5 us
  blocking collectives: 19.5 us -> 0 us
  other arithmetic: 15 us -> 1.12 us
  between operations: 15.6 us -> 1.95 us
  matrix products: 11.9 us -> 0 us
  local copies, waits for them, and re-layouts: 15.9 us -> 7.89 us
    pallas_call x0 -> x1, Pallas kernels: none -> 35.5 us  [on_device(): pl.pallas_call(functools.partial(kernel, n_set, n_seq), out_shape=(jax.Sh...]
    all_gather x1 -> x0, waiting for transfers between devices: 25 us -> none  [on_device(): slice_part = lax.all_gather(local_rows, 'seq', axis=0, tiled=True)]
    reduce_scatter x1 -> x0, waiting for transfers between devices: 16.9 us -> none  [on_device(): lax.psum_scatter(jnp.dot(normed, key_value_weight, preferred_element_type...]
    dot_general x5 -> x0, matrix products: 11.9 us -> none  [the longest x2 5.55 us: attend(): jnp.einsum('tgkn,ngd->tgkd', weights.astype(jnp.bfloat16), value_matrix,...]
    psum x1 -> x0, blocking collectives: 10.8 us -> none  [on_device(): squares = lax.psum(jnp.sum(hidden * hidden, axis=1), 'seq')]
    all_gather x1 -> x0, blocking collectives: 8.7 us -> none  [on_device(): joined_rows = lax.all_gather(block_kv, 'set', axis=1, tiled=True)]
    reduce_sum x3 -> x0, other arithmetic: 5.74 us -> none  [the longest x2 4.09 us: attend(): total = total * shrink + jnp.sum(weights, axis=-1)]
    convert_element_type x6 -> x0, other arithmetic: 4.33 us -> none  [the longest x1 1.46 us: on_device(): query_rows = apply_rotary(cont_query[0].astype(jnp.float32).reshape(step_...]
  transfers between devices with their start and end apart: 2 -> 0, of which waited for: 2 -> 0; matrix products, arithmetic and copies ran while one was open for 7% -> 0% of each run, Pallas kernels for 0% -> 0%
where the time goes in v1:
time: 46.8 us; the launch traced here: 46.4 us
  Pallas kernels  35.5 us (76%)
  local copies, waits for them, and re-layouts  7.89 us (17%)
  between operations  1.95 us (4%)
  other arithmetic  1.12 us (2%)
    pallas_call x1, Pallas kernels, on_device(): pl.pallas_call(functools.partial(kernel, n_set, n_seq), out_shape=(jax.Sh...  35.5 us
    unnamed x15, local copies, waits for them, and re-layouts  7.89 us
    broadcast_in_dim x1, other arithmetic, on_device(): jnp.where(live[:, None], attended, 0.0).astype(BF16)[None]  1.11 us

profile of v1, /device:TPU:1, one launch (start us, length us, event | category | flops | bytes accessed | tf_op | source)
XLA Modules:
  0.0 46.4 jit_solution(10937573542654260058)
XLA Ops:
  1.9 0.0 copy-start
  1.9 1.6 %copy-done = bf16[2048,512]{1,0:T(8,128)(2,1)S(1)} copy-done((bf16[2048,512]{1,0:T(8,128)(2,1)S(1)}, bf16[2048,512]{1,0:T(8,128)(2,1)}, u32[]{:S(2)}) %copy-start) | copy-done | bytes 2097176
  3.5 0.0 copy-start.1
  3.5 1.2 %copy-done.1 = bf16[256,2048]{1,0:T(8,128)(2,1)S(1)} copy-done((bf16[256,2048]{1,0:T(8,128)(2,1)S(1)}, bf16[256,2048]{1,0:T(8,128)(2,1)}, u32[]{:S(2)}) %copy-start.1) | copy-done | bytes 1048600
  4.8 0.0 copy-start.2
  4.8 1.2 %copy-done.2 = bf16[1,64,8192]{2,1,0:T(8,128)(2,1)S(1)} copy-done((bf16[1,64,8192]{2,1,0:T(8,128)(2,1)S(1)}, bf16[1,64,8192]{2,1,0:T(8,128)(2,1)}, u32[]{:S(2)}) %copy-start.2) | copy-done | bytes 1048600
  6.0 0.0 copy-start.3
  6.0 0.9 %copy-done.3 = bf16[1,64,2048]{2,1,0:T(8,128)(2,1)S(1)} copy-done((bf16[1,64,2048]{2,1,0:T(8,128)(2,1)S(1)}, bf16[1,64,2048]{2,1,0:T(8,128)(2,1)}, u32[]{:S(2)}) %copy-start.3) | copy-done | bytes 262168
  6.9 0.0 copy-start.4
  6.9 0.9 %copy-done.4 = bf16[32,2048]{1,0:T(8,128)(2,1)S(1)} copy-done((bf16[32,2048]{1,0:T(8,128)(2,1)S(1)}, bf16[32,2048]{1,0:T(8,128)(2,1)}, u32[]{:S(2)}) %copy-start.4) | copy-done | bytes 131096
  7.8 0.0 copy-start.5
  7.8 0.7 %copy-done.5 = bf16[2048]{0:T(1024)(128)(2,1)S(1)} copy-done((bf16[2048]{0:T(1024)(128)(2,1)S(1)}, bf16[2048]{0:T(1024)(128)(2,1)}, u32[]{:S(2)}) %copy-start.5) | copy-done | bytes 4120
  8.5 0.0 copy-start.6
  8.5 0.7 %copy-done.6 = f32[8,128]{1,0:T(8,128)S(1)} copy-done((f32[8,128]{1,0:T(8,128)S(1)}, f32[8,128]{1,0:T(8,128)}, u32[]{:S(2)}) %copy-start.6) | copy-done | bytes 4120
  9.2 35.5 %project_gather_attend.1 = (bf16[64,512]{1,0:T(8,128)(2,1)S(1)}, bf16[64,8192]{1,0:T(8,128)(2,1)S(1)}) custom-call(bf16[256,2048]{1,0:T(8,128)(2,1)S(1)} %copy-done.1, bf16[16,128]{1,0:T(8,128)(2,1)S(1)} %bitcast.5, bf16[2048,512]{1,0:T(8,128)(2,1)S(1)} %copy-done, bf16[32,2048]{1,0:T(8,128)(2,1)S(1)} %copy-done.4, s32[1]{0:T(128)S(6)} %copy.12.offset_smem, ...), custom_call_target="tpu_custom_call" | custom-call | tf_op jit(solution)/shard_map/project_gather_attend/pallas_call | solution.py:438
  44.7 1.1 %select_bitcast_fusion = bf16[1,64,8192]{2,1,0:T(8,128)(2,1)} fusion(bf16[64,8192]{1,0:T(8,128)(2,1)S(1)} %get-tuple-element.5, pred[64]{0:T(512)(128)(4,1)S(1)} %iota_compare_fusion), kind=kLoop, calls=%fused_computation | loop fusion | flops 524288 | bytes 2097216 | tf_op jit(solution)/shard_map/broadcast_in_dim | solution.py:508
  45.8 0.6 %copy.14 = bf16[64,512]{1,0:T(8,128)(2,1)} copy(bf16[64,512]{1,0:T(8,128)(2,1)S(1)} %get-tuple-element.8) | data formatting | bytes 131072
  (1 shorter events, 0.0 us)
Async XLA Ops:
  1.9 1.6 %copy-start = (bf16[2048,512]{1,0:T(8,128)(2,1)S(1)}, bf16[2048,512]{1,0:T(8,128)(2,1)}, u32[]{:S(2)}) copy-start(bf16[2048,512]{1,0:T(8,128)(2,1)} %weight_hbm.1) | copy-start | bytes 6291460
  3.5 1.2 %copy-start.1 = (bf16[256,2048]{1,0:T(8,128)(2,1)S(1)}, bf16[256,2048]{1,0:T(8,128)(2,1)}, u32[]{:S(2)}) copy-start(bf16[256,2048]{1,0:T(8,128)(2,1)} %hidden_hbm.1) | copy-start | bytes 3145732
  4.8 1.2 %copy-start.2 = (bf16[1,64,8192]{2,1,0:T(8,128)(2,1)S(1)}, bf16[1,64,8192]{2,1,0:T(8,128)(2,1)}, u32[]{:S(2)}) copy-start(bf16[1,64,8192]{2,1,0:T(8,128)(2,1)} %query_hbm.1) | copy-start | bytes 3145732
  6.0 0.9 %copy-start.3 = (bf16[1,64,2048]{2,1,0:T(8,128)(2,1)S(1)}, bf16[1,64,2048]{2,1,0:T(8,128)(2,1)}, u32[]{:S(2)}) copy-start(bf16[1,64,2048]{2,1,0:T(8,128)(2,1)} %own_hbm.1) | copy-start | bytes 786436
  6.9 0.9 %copy-start.4 = (bf16[32,2048]{1,0:T(8,128)(2,1)S(1)}, bf16[32,2048]{1,0:T(8,128)(2,1)}, u32[]{:S(2)}) copy-start(bf16[32,2048]{1,0:T(8,128)(2,1)} %prompt_hbm.1) | copy-start | bytes 393220
  7.8 0.7 %copy-start.5 = (bf16[2048]{0:T(1024)(128)(2,1)S(1)}, bf16[2048]{0:T(1024)(128)(2,1)}, u32[]{:S(2)}) copy-start(bf16[2048]{0:T(1024)(128)(2,1)} %param.10) | copy-start | bytes 12292
  8.5 0.7 %copy-start.6 = (f32[8,128]{1,0:T(8,128)S(1)}, f32[8,128]{1,0:T(8,128)}, u32[]{:S(2)}) copy-start(f32[8,128]{1,0:T(8,128)} %constant.5.clone.frequency_hbm) | copy-start | bytes 12292

commit v2 on v1

--- a/solution.py
+++ b/solution.py
@@ -88,6 +88,8 @@
     query,
     best,
     accum,
+    outgoing,
+    store_sem,
     load_sem,
     span_store_sem,
     square_send,
@@ -150,9 +152,6 @@
         load(weight_hbm.at[:, pl.ds(i * half, half)], weight.at[:, pl.ds(i * half, half)])
         for i in range(halves)
     ]
-    frequency_load = load(frequency_hbm, frequency)
-    own_load = load(own_hbm.at[0], own)
-    query_load = load(query_hbm.at[0], query_in)
 
     barrier = pltpu.get_barrier_semaphore()
     partners = [{"seq": seq_at(d)} for d in range(1, n_seq)]
@@ -160,6 +159,46 @@
     partners += [{"set": twin}]
     for partner in partners:
         pl.semaphore_signal(barrier, inc=1, device_id=partner, device_id_type=MESH)
+    for copy in prompt_loads:
+        copy.wait()
+    pl.semaphore_wait(barrier, len(partners))
+
+    copies = []
+
+    def remote(source, target, send_sem, recv_sem, device):
+        return pltpu.make_async_remote_copy(
+            src_ref=source,
+            dst_ref=target,
+            send_sem=send_sem,
+            recv_sem=recv_sem,
+            device_id=device,
+            device_id_type=MESH,
+        )
+
+    def send(*args):
+        copy = remote(*args)
+        copy.start()
+        copies.append(copy)
+        return copy
+
+    def other_seq(j):
+        upper = (2 * me_seq) // n_seq
+        low = j + (j - me_seq + n_seq) // n_seq
+        down = n_seq - 1 - j
+        high = down - (me_seq - down + n_seq) // n_seq
+        return low + upper * (high - low)
+
+    others = range(n_seq - 1)
+
+    def prompt_block(s, z):
+        return prompt.at[s, rows_of(z, cached), :]
+
+    def span_block(s, i, z):
+        return span.at[s * halves + i, rows_of(z, rows), :]
+
+    for j in reversed(others):
+        block, z = prompt_block(me_set, me_seq), other_seq(j)
+        send(block, block, pz_send.at[z], pz_recv.at[me_seq], {"seq": z})
 
     hidden_load.wait()
     gain_load.wait()
@@ -173,65 +212,50 @@
     square_row = jnp.sum(squares.T, axis=0, keepdims=True)
     square_mine[...] = jnp.broadcast_to(square_row, square_mine.shape)
 
-    for copy in prompt_loads:
-        copy.wait()
-    pl.semaphore_wait(barrier, len(partners))
-
-    copies = []
-
-    def send(source, target, send_sem, recv_sem, device):
-        copy = pltpu.make_async_remote_copy(
-            src_ref=source,
-            dst_ref=target,
-            send_sem=send_sem,
-            recv_sem=recv_sem,
-            device_id=device,
-            device_id_type=MESH,
-        )
-        copy.start()
-        copies.append(copy)
-        return copy
-
-    def prompt_block(s, z):
-        return prompt.at[s, rows_of(z, cached), :]
-
-    def span_block(s, z):
-        return span.at[s, rows_of(z, rows), :]
-
-    prompt_z = []
-    for d in range(1, n_seq):
-        block = prompt_block(me_set, me_seq)
-        prompt_z.append(
-            send(block, block, pz_send.at[d], pz_recv.at[d], {"seq": seq_at(d)})
-        )
-    square_copies = [
-        send(
-            square_mine,
-            square_theirs.at[d],
-            square_send.at[d],
-            square_recv.at[d],
-            {"seq": seq_at(d)},
-        )
-        for d in range(1, n_seq)
-    ]
-
-    part_copies = []
     for i in range(halves):
         weight_loads[i].wait()
+        if i == 0:
+            for j in reversed(others):
+                z = other_seq(j)
+                send(
+                    square_mine,
+                    square_theirs.at[me_seq],
+                    square_send.at[z],
+                    square_recv.at[me_seq],
+                    {"seq": z},
+                )
         columns = pl.ds(i * half, half)
         product = jnp.dot(scaled[...], weight[:, columns], preferred_element_type=F32)
         partial[:, columns] = product
         sending[i] = product.astype(BF16)
-        for d in range(1, n_seq):
-            part_copies.append(
-                send(
-                    sending.at[i, rows_of(seq_at(d), rows), :],
-                    received.at[i, d],
-                    part_send.at[i, d],
-                    part_recv.at[i, d],
-                    {"seq": seq_at(d)},
-                )
+        for j in reversed(others):
+            z = other_seq(j)
+            send(
+                sending.at[i, rows_of(z, rows), :],
+                received.at[i, me_seq],
+                part_send.at[i, z],
+                part_recv.at[i, me_seq],
+                {"seq": z},
             )
+
+    own_load = load(own_hbm.at[0], own)
+    query_load = load(query_hbm.at[0], query_in)
+    frequency_load = load(frequency_hbm, frequency)
+
+    def pass_prompt(j):
+        z = other_seq(j)
+        block = prompt_block(me_set, z)
+        remote(block, block, pz_send.at[z], pz_recv.at[z], {"seq": z}).wait_recv()
+        for e in range(1, n_x):
+            send(block, block, px_send.at[z, e], px_recv.at[z, e], {"set": set_at(e)})
+        send(block, block, pc_send.at[z, 0], pc_recv.at[z, 0], {"set": twin})
+
+    def pass_prompt_twin(j):
+        z = other_seq(j)
+        for e in range(1, n_x):
+            come = prompt_block(set_at(n_x - e), z)
+            remote(come, come, px_send.at[z, e], px_recv.at[z, e], {"set": twin}).wait_recv()
+            send(come, come, pc_send.at[z, e], pc_recv.at[z, e], {"set": twin})
 
     frequency_load.wait()
     offset = offset_smem[0]
@@ -265,150 +289,180 @@
         accum[head] = jnp.dot(weights, with_ones(values), preferred_element_type=F32)
         return carry
 
-    def pass_prompt(d):
-        prompt_z[d - 1].wait_recv()
-        block = prompt_block(me_set, seq_at(n_seq - d))
-        for e in range(1, n_x):
-            send(block, block, px_send.at[d, e], px_recv.at[d, e], {"set": set_at(e)})
-        send(block, block, pc_send.at[d, 0], pc_recv.at[d, 0], {"set": twin})
-
-    def pass_prompt_twin(d):
-        block = prompt_block(me_set, seq_at(n_seq - d))
-        for e in range(1, n_x):
-            pltpu.make_async_remote_copy(
-                block, block, px_send.at[d, e], px_recv.at[d, e], {"set": set_at(e)}, MESH
-            ).wait_recv()
-            come = prompt_block(set_at(n_x - e), seq_at(n_seq - d))
-            send(come, come, pc_send.at[d, e], pc_recv.at[d, e], {"set": twin})
-
     lax.fori_loop(0, KEY_HEADS // 4, attend_own, 0)
-    for d in range(1, n_seq):
-        pass_prompt(d)
+    for j in others:
+        pass_prompt(j)
     lax.fori_loop(KEY_HEADS // 4, KEY_HEADS, attend_own, 0)
-    for d in range(1, n_seq):
-        pass_prompt_twin(d)
-
-    for copy in square_copies:
-        copy.wait_recv()
+    for j in others:
+        pass_prompt_twin(j)
+
     square_total = square_mine[...]
-    for d in range(1, n_seq):
-        square_total += square_theirs[d]
+    for j in others:
+        z = other_seq(j)
+        remote(
+            square_mine, square_theirs.at[z], square_send.at[z], square_recv.at[z], {"seq": z}
+        ).wait_recv()
+        square_total += square_theirs[z]
     square_column[...] = jnp.broadcast_to(
         square_total[0:1, :], (HEAD_SIZE, square_total.shape[1])
     ).T
     inverse = lax.rsqrt(square_column[rows_of(me_seq, rows), :] / MODEL_WIDTH + EPS)
-    for copy in part_copies:
-        copy.wait_recv()
-    for i in range(halves):
-        for j in range(half // HEAD_SIZE):
-            column = i * half + j * HEAD_SIZE
+
+    def finish(i):
+        for j in others:
+            z = other_seq(j)
+            remote(
+                sending.at[i, rows_of(z, rows), :],
+                received.at[i, z],
+                part_send.at[i, z],
+                part_recv.at[i, z],
+                {"seq": z},
+            ).wait_recv()
+        for c in range(half // HEAD_SIZE):
+            column = i * half + c * HEAD_SIZE
             block = partial[rows_of(me_seq, rows), pl.ds(column, HEAD_SIZE)]
-            for d in range(1, n_seq):
-                block += received[i, d, :, pl.ds(j * HEAD_SIZE, HEAD_SIZE)].astype(F32)
+            for j in others:
+                block += received[i, other_seq(j), :, pl.ds(c * HEAD_SIZE, HEAD_SIZE)].astype(F32)
             block = block * inverse
             turned = turn(block, span_cosine, span_sine)
             is_key = me_set * width + column < KEY_COLUMNS
-            span[me_set, rows_of(me_seq, rows), pl.ds(column, HEAD_SIZE)] = jnp.where(
-                is_key, turned, block
-            ).astype(BF16)
-
-    mine = span_block(me_set, me_seq)
-    span_z = []
-    sx, sc = {}, {}
-    for e in range(1, n_x):
-        sx[0, e] = send(mine, mine, sx_send.at[0, e], sx_recv.at[0, e], {"set": set_at(e)})
-    for d in range(1, n_seq):
-        span_z.append(send(mine, mine, sz_send.at[d], sz_recv.at[d], {"seq": seq_at(d)}))
-    send(mine, mine, sc_send.at[0, 0], sc_recv.at[0, 0], {"set": twin})
-    span_store = pltpu.make_async_copy(mine, span_out, span_store_sem)
-    span_store.start()
-
-    def pass_span(d):
-        span_z[d - 1].wait_recv()
-        block = span_block(me_set, seq_at(n_seq - d))
+            span[
+                me_set * halves + i, rows_of(me_seq, rows), pl.ds(c * HEAD_SIZE, HEAD_SIZE)
+            ] = jnp.where(is_key, turned, block).astype(BF16)
+        mine = span_block(me_set, i, me_seq)
         for e in range(1, n_x):
-            sx[d, e] = send(
-                block, block, sx_send.at[d, e], sx_recv.at[d, e], {"set": set_at(e)}
+            send(
+                mine, mine, sx_send.at[i, me_seq, e], sx_recv.at[i, me_seq, e], {"set": set_at(e)}
             )
-        send(block, block, sc_send.at[d, 0], sc_recv.at[d, 0], {"set": twin})
-
-    def pass_span_twin(d):
+        for j in others:
+            z = other_seq(j)
+            send(mine, mine, sz_send.at[i, z], sz_recv.at[i, me_seq], {"seq": z})
+        send(mine, mine, sc_send.at[i, me_seq, 0], sc_recv.at[i, me_seq, 0], {"set": twin})
+        span_store(i).start()
+
+    def span_store(i):
+        return pltpu.make_async_copy(
+            span_block(me_set, i, me_seq),
+            span_out.at[:, pl.ds(i * half, half)],
+            span_store_sem.at[i],
+        )
+
+    def pass_span(i, j):
+        z = other_seq(j)
+        block = span_block(me_set, i, z)
+        remote(block, block, sz_send.at[i, z], sz_recv.at[i, z], {"seq": z}).wait_recv()
         for e in range(1, n_x):
-            sx[d, e].wait_recv()
-            come = span_block(set_at(n_x - e), seq_at(n_seq - d))
-            send(come, come, sc_send.at[d, e], sc_recv.at[d, e], {"set": twin})
+            send(block, block, sx_send.at[i, z, e], sx_recv.at[i, z, e], {"set": set_at(e)})
+        send(block, block, sc_send.at[i, z, 0], sc_recv.at[i, z, 0], {"set": twin})
+
+    def pass_span_twin(i, z):
+        for e in range(1, n_x):
+            come = span_block(set_at(n_x - e), i, z)
+            remote(
+                come, come, sx_send.at[i, z, e], sx_recv.at[i, z, e], {"set": twin}
+            ).wait_recv()
+            send(come, come, sc_send.at[i, z, e], sc_recv.at[i, z, e], {"set": twin})
+
+    def span_arrived(i):
+        twin_x = twin
+        for z in range(n_seq):
+            for e in range(n_x):
+                come = span_block(twin_x, i, z)
+                remote(
+                    come, come, sc_send.at[i, z, e], sc_recv.at[i, z, e], {"set": twin}
+                ).wait_recv()
 
     def attend_more(head, keys, values, mask):
         scores = scores_of(query[head], keys)
         if mask is not None:
             scores = jnp.where(mask, scores, NEGATIVE_LARGE)
-        old = best[head][:, 0:1]
+        old = best[head]
         top = jnp.maximum(old, jnp.max(scores, axis=1, keepdims=True))
-        weights = jnp.exp2((scores - top) * EXPONENT).astype(BF16)
+        spread = jnp.concatenate([top] * (scores.shape[1] // HEAD_SIZE), axis=1)
+        weights = jnp.exp2((scores - spread) * EXPONENT).astype(BF16)
         shrink = jnp.exp2((old - top) * EXPONENT)
-        total = accum[head] * shrink + jnp.dot(
+        total = accum[head] * jnp.concatenate([shrink, shrink], axis=1) + jnp.dot(
             weights, with_ones(values), preferred_element_type=F32
         )
         return top, total
 
     per_set = width // HEAD_SIZE
-
-    def head_of(array, head):
-        return array[head // per_set, :, columns_of(head % per_set)]
-
-    live = (
-        lax.broadcasted_iota(jnp.int32, (1, prompt.shape[1]), 1) < offset
-    )
+    per_part = half // HEAD_SIZE
+    live = lax.broadcasted_iota(jnp.int32, (1, prompt.shape[1]), 1) < offset
+
+    def prompt_head(head):
+        return prompt[head // per_set, :, columns_of(head % per_set)]
+
+    def span_head(head):
+        start = head % per_part * HEAD_SIZE
+        return span[head // per_part, :, start : start + HEAD_SIZE]
 
     def attend_prompt(head, carry):
-        top, total = attend_more(
-            head, head_of(prompt, head), head_of(prompt, head + KEY_HEADS), live
-        )
-        best[head] = jnp.broadcast_to(top, best.shape[1:])
+        top, total = attend_more(head, prompt_head(head), prompt_head(head + KEY_HEADS), live)
+        best[head] = top
         accum[head] = total
         return carry
 
-    for d in range(1, n_seq):
-        for e in range(n_x):
-            pltpu.make_async_remote_copy(
-                prompt_block(me_set, me_seq),
-                prompt_block(me_set, me_seq),
-                pc_send.at[d, e],
-                pc_recv.at[d, e],
-                {"set": twin},
-                MESH,
-            ).wait_recv()
-    cut = [KEY_HEADS * d // n_seq for d in range(n_seq + 1)]
-    lax.fori_loop(cut[0], cut[1], attend_prompt, 0)
-    pass_span_twin(0)
-    for d in range(1, n_seq):
-        pass_span(d)
-        if cut[d] < cut[d + 1]:
-            lax.fori_loop(cut[d], cut[d + 1], attend_prompt, 0)
-    for d in range(1, n_seq):
-        pass_span_twin(d)
-    for d in range(n_seq):
-        for e in range(n_x):
-            pltpu.make_async_remote_copy(
-                mine, mine, sc_send.at[d, e], sc_recv.at[d, e], {"set": twin}, MESH
-            ).wait_recv()
-
-    def attend_span(head, carry):
-        top, total = attend_more(
-            head, head_of(span, head), head_of(span, head + KEY_HEADS), None
+    def store_of(head):
+        columns = pl.ds(head * GROUP * HEAD_SIZE, GROUP * HEAD_SIZE)
+        return pltpu.make_async_copy(
+            outgoing.at[:, columns], attended_out.at[:, columns], store_sem.at[head]
         )
+
+    def attend_span(head):
+        top, total = attend_more(head, span_head(head), span_head(head + KEY_HEADS), None)
         mixed = (total[:, :HEAD_SIZE] / total[:, HEAD_SIZE:]).astype(BF16)
         for g in range(GROUP):
-            attended_out[:, columns_of(head * GROUP + g)] = mixed[
-                g * tokens : (g + 1) * tokens, :
-            ]
-        return carry
-
-    lax.fori_loop(0, KEY_HEADS, attend_span, 0)
+            column = (head * GROUP + g) * HEAD_SIZE
+            outgoing[:, column : column + HEAD_SIZE] = mixed[g * tokens : (g + 1) * tokens, :]
+        store_of(head).start()
+
+    def prompt_arrived():
+        for j in others:
+            z = other_seq(j)
+            for e in range(n_x):
+                come = prompt_block(twin, z)
+                remote(
+                    come, come, pc_send.at[z, e], pc_recv.at[z, e], {"set": twin}
+                ).wait_recv()
+
+    finish(0)
+    prompt_arrived()
+    middle = KEY_HEADS // 2
+    lax.fori_loop(0, middle, attend_prompt, 0)
+    for i in range(1, halves):
+        finish(i)
+    pass_span_twin(0, me_seq)
+    for j in others:
+        pass_span(0, j)
+        cut = [middle + (KEY_HEADS - middle) * k // (n_seq - 1) for k in (j, j + 1)]
+        if cut[0] < cut[1]:
+            lax.fori_loop(cut[0], cut[1], attend_prompt, 0)
+    for j in others:
+        pass_span_twin(0, other_seq(j))
+    for i in range(halves):
+        heads = [h for h in range(KEY_HEADS) if h % per_set // per_part == i]
+        steps = []
+        if i + 1 < halves:
+            steps = [functools.partial(pass_span_twin, i + 1, me_seq)]
+            steps += [functools.partial(pass_span, i + 1, j) for j in others]
+        for step in steps[:3]:
+            step()
+        span_arrived(i)
+        for step in steps[3:]:
+            step()
+        for head in heads:
+            attend_span(head)
+        if i + 1 < halves:
+            for j in others:
+                pass_span_twin(i + 1, other_seq(j))
 
     for copy in copies:
         copy.wait_send()
-    span_store.wait()
+    for i in range(halves):
+        span_store(i).wait()
+    for head in range(KEY_HEADS):
+        store_of(head).wait()
 
 
 def on_device(
@@ -451,7 +505,7 @@
             anywhere,
             anywhere,
         ],
-        out_specs=(anywhere, pl.BlockSpec(memory_space=pltpu.VMEM)),
+        out_specs=(anywhere, anywhere),
         scratch_shapes=[
             pltpu.VMEM((span_length, features), BF16),
             pltpu.VMEM((features // HEAD_SIZE, HEAD_SIZE), BF16),
@@ -467,12 +521,14 @@
             pltpu.VMEM((8, span_length), F32),
             pltpu.VMEM((n_seq, 8, span_length), F32),
             pltpu.VMEM((span_length, HEAD_SIZE), F32),
-            pltpu.VMEM((n_set, span_length, width), BF16),
+            pltpu.VMEM((n_set * halves, span_length, half), BF16),
             pltpu.VMEM((KEY_HEADS, GROUP * tokens, HEAD_SIZE), BF16),
             pltpu.VMEM((KEY_HEADS, GROUP * tokens, HEAD_SIZE), F32),
             pltpu.VMEM((KEY_HEADS, GROUP * tokens, 2 * HEAD_SIZE), F32),
+            pltpu.VMEM((tokens, QUERY_HEADS * HEAD_SIZE), BF16),
+            dma((KEY_HEADS,)),
             dma((n_set + halves + 5,)),
-            dma,
+            dma((halves,)),
             dma((n_seq,)),
             dma((n_seq,)),
             dma((halves, n_seq)),
@@ -483,15 +539,15 @@
             dma((n_seq, n_x)),
             dma((n_seq, n_x)),
             dma((n_seq, n_x)),
-            dma((n_seq,)),
-            dma((n_seq,)),
-            dma((n_seq, n_x)),
-            dma((n_seq, n_x)),
-            dma((n_seq, n_x)),
-            dma((n_seq, n_x)),
+            dma((halves, n_seq)),
+            dma((halves, n_seq)),
+            dma((halves, n_seq, n_x)),
+            dma((halves, n_seq, n_x)),
+            dma((halves, n_seq, n_x)),
+            dma((halves, n_seq, n_x)),
         ],
         compiler_params=pltpu.CompilerParams(
-            collective_id=0, has_side_effects=True, vmem_limit_bytes=48 * 1024 * 1024
+            collective_id=0, has_side_effects=True, vmem_limit_bytes=67043328
         ),
         name="project_gather_attend",
     )(

time: 46.8 us -> 37 us (0.79)
  local copies, waits for them, and re-layouts: 7.89 us -> 0.63 us
  Pallas kernels: 35.5 us -> 31.3 us
  other arithmetic: 1.12 us -> 2.95 us
    unnamed x15 -> x3, local copies, waits for them, and re-layouts: 7.89 us -> 0.63 us
    pallas_call x1, Pallas kernels: 35.5 us -> 31.3 us  [on_device(): pl.pallas_call(functools.partial(kernel, n_set, n_seq), out_shape=(jax.Sh...]
    broadcast_in_dim x1, other arithmetic: 1.11 us -> 2.37 us  [on_device(): jnp.where(live[:, None], attended, 0.0).astype(BF16)[None]]
    lt x1, other arithmetic: 0.01 us -> 0.58 us  [on_device(): live = jnp.arange(tokens, dtype=jnp.int32) < cont_lengths[0]]
where the time goes in v2:
time: 37 us; the launch traced here: 36.8 us
  Pallas kernels  31.3 us (85%)
  other arithmetic  2.95 us (8%)
  between operations  1.94 us (5%)
  local copies, waits for them, and re-layouts  0.63 us (2%)
    pallas_call x1, Pallas kernels, on_device(): pl.pallas_call(functools.partial(kernel, n_set, n_seq), out_shape=(jax.Sh...  31.3 us
    broadcast_in_dim x1, other arithmetic, on_device(): jnp.where(live[:, None], attended, 0.0).astype(BF16)[None]  2.37 us

profile of v2, /device:TPU:1, one launch (start us, length us, event | category | flops | bytes accessed | tf_op | source)
XLA Modules:
  0.0 36.8 jit_solution(17071848227817265808)
XLA Ops:
  1.9 0.6 %iota_compare_fusion = pred[64]{0:T(512)(128)(4,1)} fusion(s32[]{:T(128)} %bitcast.4), kind=kLoop, calls=%fused_computation.1 | loop fusion | flops 64 | bytes 68 | tf_op jit(solution)/shard_map/lt | solution.py:563
  2.5 31.3 %project_gather_attend.1 = (bf16[64,512]{1,0:T(8,128)(2,1)}, bf16[64,8192]{1,0:T(8,128)(2,1)}) custom-call(bf16[256,2048]{1,0:T(8,128)(2,1)} %hidden_hbm.1, bf16[16,128]{1,0:T(8,128)(2,1)} %bitcast.5, bf16[2048,512]{1,0:T(8,128)(2,1)} %weight_hbm.1, bf16[32,2048]{1,0:T(8,128)(2,1)} %prompt_hbm.1, s32[1]{0:T(128)S(6)} %copy.12.offset_smem, ...), custom_call_target="tpu_custom_call" | custom-call | tf_op jit(solution)/shard_map/project_gather_attend/pallas_call | solution.py:492
  33.8 0.0 copy-start
  33.8 2.4 %select_bitcast_fusion = bf16[1,64,8192]{2,1,0:T(8,128)(2,1)} fusion(bf16[64,8192]{1,0:T(8,128)(2,1)} %get-tuple-element.5, pred[64]{0:T(512)(128)(4,1)} %iota_compare_fusion), kind=kLoop, calls=%fused_computation | loop fusion | flops 524288 | bytes 2097216 | tf_op jit(solution)/shard_map/broadcast_in_dim | solution.py:564
  36.1 0.0 copy-done
  36.1 0.6 %copy.14 = bf16[64,512]{1,0:T(8,128)(2,1)} copy(bf16[64,512]{1,0:T(8,128)(2,1)S(1)} %copy-done) | data formatting | bytes 131072
Async XLA Ops:
  33.8 2.4 %copy-start = (bf16[64,512]{1,0:T(8,128)(2,1)S(1)}, bf16[64,512]{1,0:T(8,128)(2,1)}, u32[]{:S(2)}) copy-start(bf16[64,512]{1,0:T(8,128)(2,1)} %get-tuple-element.8) | copy-start | bytes 196612

commit v3 on v2

--- a/solution.py
+++ b/solution.py
@@ -65,6 +65,7 @@
     weight_hbm,
     prompt_hbm,
     offset_smem,
+    length_smem,
     query_hbm,
     own_hbm,
     frequency_hbm,
@@ -386,6 +387,7 @@
         )
         return top, total
 
+    kept = lax.broadcasted_iota(jnp.int32, (tokens, HEAD_SIZE), 0) < length_smem[0]
     per_set = width // HEAD_SIZE
     per_part = half // HEAD_SIZE
     live = lax.broadcasted_iota(jnp.int32, (1, prompt.shape[1]), 1) < offset
@@ -411,10 +413,12 @@
 
     def attend_span(head):
         top, total = attend_more(head, span_head(head), span_head(head + KEY_HEADS), None)
-        mixed = (total[:, :HEAD_SIZE] / total[:, HEAD_SIZE:]).astype(BF16)
+        mixed = total[:, :HEAD_SIZE] / total[:, HEAD_SIZE:]
         for g in range(GROUP):
             column = (head * GROUP + g) * HEAD_SIZE
-            outgoing[:, column : column + HEAD_SIZE] = mixed[g * tokens : (g + 1) * tokens, :]
+            outgoing[:, column : column + HEAD_SIZE] = jnp.where(
+                kept, mixed[g * tokens : (g + 1) * tokens, :], 0.0
+            ).astype(BF16)
         store_of(head).start()
 
     def prompt_arrived():
@@ -463,6 +467,26 @@
         span_store(i).wait()
     for head in range(KEY_HEADS):
         store_of(head).wait()
+
+
+def hand_on(chunks, span_in, attended_in, span_out, attended_out, rows, tokens, in_sem, out_sem):
+    step = tokens.shape[0] // chunks
+    parts = [pl.ds(c * step, step) for c in range(chunks)]
+    ins = [
+        pltpu.make_async_copy(attended_in.at[part, :], tokens.at[part, :], in_sem.at[c])
+        for c, part in enumerate(parts)
+    ] + [pltpu.make_async_copy(span_in, rows, in_sem.at[chunks])]
+    outs = [
+        pltpu.make_async_copy(tokens.at[part, :], attended_out.at[0, part, :], out_sem.at[c])
+        for c, part in enumerate(parts)
+    ] + [pltpu.make_async_copy(rows, span_out, out_sem.at[chunks])]
+    for copy in ins:
+        copy.start()
+    for arriving, leaving in zip(ins, outs):
+        arriving.wait()
+        leaving.start()
+    for copy in outs:
+        copy.wait()
 
 
 def on_device(
@@ -500,6 +524,7 @@
             anywhere,
             anywhere,
             anywhere,
+            pl.BlockSpec(memory_space=pltpu.SMEM),
             pl.BlockSpec(memory_space=pltpu.SMEM),
             anywhere,
             anywhere,
@@ -556,12 +581,29 @@
         key_value_weight,
         prompt_key_value,
         span_offset,
+        cont_lengths,
         cont_query,
         continuation_key_value,
         frequency,
     )
-    live = jnp.arange(tokens, dtype=jnp.int32) < cont_lengths[0]
-    return span_rows, jnp.where(live[:, None], attended, 0.0).astype(BF16)[None]
+    chunks = 8
+    return pl.pallas_call(
+        functools.partial(hand_on, chunks),
+        out_shape=(
+            jax.ShapeDtypeStruct((rows, width), BF16),
+            jax.ShapeDtypeStruct((1, tokens, QUERY_HEADS * HEAD_SIZE), BF16),
+        ),
+        in_specs=[anywhere, anywhere],
+        out_specs=(anywhere, anywhere),
+        scratch_shapes=[
+            pltpu.VMEM((rows, width), BF16),
+            pltpu.VMEM((tokens, QUERY_HEADS * HEAD_SIZE), BF16),
+            dma((chunks + 1,)),
+            dma((chunks + 1,)),
+        ],
+        compiler_params=pltpu.CompilerParams(vmem_limit_bytes=67043328),
+        name="hand_on",
+    )(span_rows, attended)
 
 
 def solution(mesh):

time: 37 us -> 35.6 us (0.962)
  other arithmetic: 2.95 us -> 0 us
  Pallas kernels: 31.3 us -> 33.5 us
  local copies, waits for them, and re-layouts: 0.63 us -> 0 us
    broadcast_in_dim x1 -> x0, other arithmetic: 2.37 us -> none  [on_device(): jnp.where(live[:, None], attended, 0.0).astype(BF16)[None]]
    pallas_call x0 -> x1, Pallas kernels: none -> 2.12 us  [on_device(): pl.pallas_call(functools.partial(hand_on, chunks), out_shape=(jax.ShapeDt...]
    unnamed x3 -> x0, local copies, waits for them, and re-layouts: 0.63 us -> none
    lt x1 -> x0, other arithmetic: 0.58 us -> none  [on_device(): live = jnp.arange(tokens, dtype=jnp.int32) < cont_lengths[0]]
where the time goes in v3:
time: 35.6 us; the launch traced here: 35.4 us
  Pallas kernels  33.5 us (94%)
  between operations  1.93 us (5%)
    pallas_call x1, Pallas kernels, on_device(): pl.pallas_call(functools.partial(kernel, n_set, n_seq), out_shape=(jax.Sh...  31.4 us
    pallas_call x1, Pallas kernels, on_device(): pl.pallas_call(functools.partial(hand_on, chunks), out_shape=(jax.ShapeDt...  2.12 us

profile of v3, /device:TPU:1, one launch (start us, length us, event | category | flops | bytes accessed | tf_op | source)
XLA Modules:
  0.0 35.4 jit_solution(7704878458003814753)
XLA Ops:
  1.9 31.4 %project_gather_attend.1 = (bf16[64,512]{1,0:T(8,128)(2,1)}, bf16[64,8192]{1,0:T(8,128)(2,1)}) custom-call(bf16[256,2048]{1,0:T(8,128)(2,1)} %hidden_hbm.1, bf16[16,128]{1,0:T(8,128)(2,1)} %bitcast.1, bf16[2048,512]{1,0:T(8,128)(2,1)} %weight_hbm.1, bf16[32,2048]{1,0:T(8,128)(2,1)} %prompt_hbm.1, s32[1]{0:T(128)S(6)} %copy.11.offset_smem, ...), custom_call_target="tpu_custom_call" | custom-call | tf_op jit(solution)/shard_map/project_gather_attend/pallas_call | solution.py:516
  33.3 2.1 %hand_on.1 = (bf16[64,512]{1,0:T(8,128)(2,1)}, bf16[1,64,8192]{2,1,0:T(8,128)(2,1)}) custom-call(bf16[64,512]{1,0:T(8,128)(2,1)} %get-tuple-element.4.span_in, bf16[64,8192]{1,0:T(8,128)(2,1)} %get-tuple-element.5.attended_in), custom_call_target="tpu_custom_call" | custom-call | tf_op jit(solution)/shard_map/hand_on/pallas_call | solution.py:590

commit v4 on v3

--- a/solution.py
+++ b/solution.py
@@ -450,13 +450,15 @@
         if i + 1 < halves:
             steps = [functools.partial(pass_span_twin, i + 1, me_seq)]
             steps += [functools.partial(pass_span, i + 1, j) for j in others]
-        for step in steps[:3]:
+        for step in steps[:2]:
             step()
         span_arrived(i)
-        for step in steps[3:]:
+        for k, head in enumerate(heads):
+            attend_span(head)
+            if 2 + k < len(steps):
+                steps[2 + k]()
+        for step in steps[2 + len(heads) :]:
             step()
-        for head in heads:
-            attend_span(head)
         if i + 1 < halves:
             for j in others:
                 pass_span_twin(i + 1, other_seq(j))

time: 35.6 us -> 36.1 us (1.014)
  no operation moved by 1% of the time
where the time goes in v4:
time: 36.1 us; the launch traced here: 35.7 us
  Pallas kernels  33.8 us (94%)
  between operations  1.93 us (5%)
    pallas_call x1, Pallas kernels, on_device(): pl.pallas_call(functools.partial(kernel, n_set, n_seq), out_shape=(jax.Sh...  31.7 us
    pallas_call x1, Pallas kernels, on_device(): pl.pallas_call(functools.partial(hand_on, chunks), out_shape=(jax.ShapeDt...  2.12 us

profile of v4, /device:TPU:1, one launch (start us, length us, event | category | flops | bytes accessed | tf_op | source)
XLA Modules:
  0.0 35.7 jit_solution(4178420490838386621)
XLA Ops:
  1.9 31.7 %project_gather_attend.1 = (bf16[64,512]{1,0:T(8,128)(2,1)}, bf16[64,8192]{1,0:T(8,128)(2,1)}) custom-call(bf16[256,2048]{1,0:T(8,128)(2,1)} %hidden_hbm.1, bf16[16,128]{1,0:T(8,128)(2,1)} %bitcast.1, bf16[2048,512]{1,0:T(8,128)(2,1)} %weight_hbm.1, bf16[32,2048]{1,0:T(8,128)(2,1)} %prompt_hbm.1, s32[1]{0:T(128)S(6)} %copy.11.offset_smem, ...), custom_call_target="tpu_custom_call" | custom-call | tf_op jit(solution)/shard_map/project_gather_attend/pallas_call | solution.py:518
  33.6 2.1 %hand_on.1 = (bf16[64,512]{1,0:T(8,128)(2,1)}, bf16[1,64,8192]{2,1,0:T(8,128)(2,1)}) custom-call(bf16[64,512]{1,0:T(8,128)(2,1)} %get-tuple-element.4.span_in, bf16[64,8192]{1,0:T(8,128)(2,1)} %get-tuple-element.5.attended_in), custom_call_target="tpu_custom_call" | custom-call | tf_op jit(solution)/shard_map/hand_on/pallas_call | solution.py:592
